TPU v7x, 32 devices: a whole 2x2x4 slice. The times are simulated.
32 devices in a mesh: fsdp: 16 (over z, x, core), dp: 2 (over y).
Axes of the slice: x: 2, y: 2, z: 4, core: 2. Of those that a mesh axis runs over, the one named last changes fastest.
Arguments:
- inputs: bfloat16 [6144, 4096], P(('fsdp', 'dp')), may hold values from -6 to 6
- grad_out: bfloat16 [6144, 14336], P(('fsdp', 'dp')), may hold values from -0.009765625 to 0.009765625
- projection: bfloat16 [4096, 128], P('fsdp'), may hold values from -0.375 to 0.375
- moment: float32 [14336, 128], P('fsdp'), may hold values from -1.5 to 1.5
- second: float32 [14336, 128], P('fsdp'), may hold values from 0.0001 to 0.001
Outputs:
- update: bfloat16 [4096, 14336], P('fsdp')
- new_moment: float32 [14336, 128], P('fsdp')
- new_second: float32 [14336, 128], P('fsdp')
All inputs are finite; a program needn't handle non-finite values.
Results may differ from a plain program's by a relative error of at most 0.0051.
Values may be sent and summed in bfloat16 or wider, within the bound.
No kernel may reach another device: no remote copies, remote signals or barrier semaphores. Data moves between devices by JAX's collectives and lax.ppermute only.
A program may use at most 64 MiB of HBM per device.

v0:
```python
import jax
import jax.numpy as jnp
from jax import lax
from jax.sharding import PartitionSpec as P

STEP = 10


def adam_step(low_rank, moment, second):
    new_moment = 0.9 * moment + 0.1 * low_rank
    new_second = 0.999 * second + 0.001 * (low_rank * low_rank)
    first_fix = 1.0 - 0.9**STEP
    second_fix = 1.0 - 0.999**STEP
    normalized = (new_moment / first_fix / (jnp.sqrt(new_second / second_fix) + 1e-08)).astype(
        jnp.bfloat16
    )
    return (new_moment, new_second, normalized)


def local(inputs, grad_out, projection, moment, second):
    projected = jnp.dot(
        inputs,
        lax.all_gather(projection, "fsdp", axis=0, tiled=True),
        preferred_element_type=jnp.float32,
    ).astype(jnp.bfloat16)
    contract = (((0,), (0,)), ((), ()))
    whole = lax.dot_general(grad_out, projected, contract, preferred_element_type=jnp.float32)
    whole = lax.psum(whole, "dp")
    low_rank = lax.psum_scatter(whole, "fsdp", scatter_dimension=0, tiled=True)
    new_moment, new_second, normalized = adam_step(low_rank, moment, second)
    expand = (((1,), (1,)), ((), ()))
    update = lax.dot_general(
        projection,
        lax.all_gather(normalized, "fsdp", axis=0, tiled=True),
        expand,
        preferred_element_type=jnp.float32,
    ).astype(jnp.bfloat16)
    return (update, new_moment, new_second)


def solution(mesh):
    in_specs = (
        P(("fsdp", "dp"), None),
        P(("fsdp", "dp"), None),
        P("fsdp", None),
        P("fsdp", None),
        P("fsdp", None),
    )
    out_specs = (P("fsdp", None), P("fsdp", None), P("fsdp", None))
    return jax.shard_map(local, mesh=mesh, in_specs=in_specs, out_specs=out_specs, check_vma=False)
```

profile of v0, /device:TPU:0, one launch (start us, length us, event | category | flops | bytes accessed | tf_op | source)
XLA Modules:
  0.0 252.6 jit_solution(8466995799311963233)
XLA Ops:
  7.2 0.0 copy-start
  7.2 0.0 all-gather.3.cloned.1.call-start
  7.2 0.7 all-gather.3.cloned.1.call-update
  7.9 0.0 reduce-scatter.2.cloned.1.call-start
  8.0 42.8 %all-gather.3.cloned.1.call-done = bf16[4096,128]{1,0:T(8,128)(2,1)} async-done(((bf16[256,128]{1,0:T(8,128)(2,1)}), bf16[4096,128]{1,0:T(8,128)(2,1)}) %all-gather.3.cloned.1.call-update) | async-done | bytes 1048592 | tf_op jit(solution)/shard_map/all_gather | solution.py:23
  50.7 0.0 copy-done
  50.7 7.6 %convolution_bitcast_fusion = f32[14336,128]{0,1:T(8,128)} fusion(bf16[192,14336]{1,0:T(8,128)(2,1)} %param.6, bf16[192,4096]{1,0:T(8,128)(2,1)S(1)} %copy-done, bf16[4096,128]{1,0:T(8,128)(2,1)} %all-gather.3.cloned.1.call-done), kind=kOutput, calls=%fused_computation.2 | convolution fusion | flops 905994240 | bytes 15466496 | tf_op jit(solution)/shard_map/dot_general | solution.py:27
  58.4 0.0 copy-start.1
  58.4 0.0 copy-start.2
  58.4 0.0 copy-start.3
  58.4 0.0 reduce-scatter.2.cloned.1.call-update
  58.4 0.0 all-reduce.2.cloned.1.call-start
  58.5 90.7 %reduce-scatter.2.cloned.1.call-done = f32[896,128]{0,1:T(8,128)} async-done(((f32[14336,128]{0,1:T(8,128)}), f32[896,128]{0,1:T(8,128)}) %reduce-scatter.2.cloned.1.call-update) | async-done | bytes 458768 | tf_op jit(solution)/shard_map/reduce_scatter | solution.py:29
  149.2 0.0 all-reduce.2.cloned.1.call-update
  149.2 0.0 all-gather.5.cloned.1.call-start
  149.3 0.0 copy-done.1
  149.3 0.2 copy.8
  149.5 0.0 copy-done.2
  149.5 0.2 copy.9
  149.7 28.8 %all-reduce.2.cloned.1.call-done = f32[896,128]{0,1:T(8,128)} async-done(((f32[896,128]{0,1:T(8,128)}), f32[896,128]{0,1:T(8,128)}) %all-reduce.2.cloned.1.call-update) | async-done | bytes 458768 | tf_op jit(solution)/shard_map/psum | solution.py:28
  178.5 2.0 divide_convert_fusion
  180.5 0.0 all-gather.5.cloned.1.call-update
  180.5 1.0 copy.11
  181.5 1.0 copy.12
  182.4 46.4 %all-gather.5.cloned.1.call-done = bf16[14336,128]{0,1:T(8,128)(2,1)} async-done(((bf16[896,128]{0,1:T(8,128)(2,1)}), bf16[14336,128]{0,1:T(8,128)(2,1)}) %all-gather.5.cloned.1.call-update) | async-done | bytes 3670032 | tf_op jit(solution)/shard_map/all_gather | solution.py:34
  228.9 0.0 copy-done.3
  228.9 7.1 %fusion = bf16[256,14336]{0,1:T(8,128)(2,1)} fusion(bf16[14336,128]{0,1:T(8,128)(2,1)} %all-gather.5.cloned.1.call-done, bf16[256,128]{1,0:T(8,128)(2,1)S(1)} %copy-done.3), kind=kOutput, calls=%fused_computation.1 | convolution fusion | flops 943194112 | bytes 11075584 | tf_op jit(solution)/shard_map/dot_general | solution.py:32
  236.0 10.1 %copy.10 = bf16[256,14336]{1,0:T(8,128)(2,1)} copy(bf16[256,14336]{0,1:T(8,128)(2,1)} %fusion) | data formatting | bytes 14680064
Async XLA Ops:
  7.2 43.6 %copy-start = (bf16[192,4096]{1,0:T(8,128)(2,1)S(1)}, bf16[192,4096]{1,0:T(8,128)(2,1)}, u32[]{:S(2)}) copy-start(bf16[192,4096]{1,0:T(8,128)(2,1)} %param.5) | copy-start | bytes 4718596
  7.2 43.6 %all-gather.3.cloned.1.call-start = ((), (), s32[]{:S(2)}) async-start(), calls=%async_computation.1 | async-start | bytes 1114112 | tf_op jit(solution)/shard_map/all_gather | solution.py:23
  7.9 141.3 %reduce-scatter.2.cloned.1.call-start = ((), (), s32[]{:S(2)}) async-start(), calls=%async_computation.3 | async-start | bytes 7798784 | tf_op jit(solution)/shard_map/reduce_scatter | solution.py:29
  58.4 90.9 %copy-start.1 = (f32[896,128]{1,0:T(8,128)S(1)}, f32[896,128]{1,0:T(8,128)}, u32[]{:S(2)}) copy-start(f32[896,128]{1,0:T(8,128)} %param.8) | copy-start | bytes 1376260
  58.4 91.1 %copy-start.2 = (f32[896,128]{1,0:T(8,128)S(1)}, f32[896,128]{1,0:T(8,128)}, u32[]{:S(2)}) copy-start(f32[896,128]{1,0:T(8,128)} %param.9) | copy-start | bytes 1376260
  58.4 170.5 %copy-start.3 = (bf16[256,128]{1,0:T(8,128)(2,1)S(1)}, bf16[256,128]{1,0:T(8,128)(2,1)}, u32[]{:S(2)}) copy-start(bf16[256,128]{1,0:T(8,128)(2,1)} %param.7) | copy-start | bytes 196612
  58.4 120.1 %all-reduce.2.cloned.1.call-start = ((), (), s32[]{:S(2)}) async-start(), calls=%async_computation.4 | async-start | bytes 917504 | tf_op jit(solution)/shard_map/psum | solution.py:28
  149.2 79.6 %all-gather.5.cloned.1.call-start = ((), (), s32[]{:S(2)}) async-start(), calls=%async_computation.2 | async-start | bytes 3899392 | tf_op jit(solution)/shard_map/all_gather | solution.py:34
Sparse Core Ops, SparseCore 0:
  10.1 40.5 all-gather.2
  58.5 90.6 reduce-scatter.1
  151.5 26.9 all-reduce.1
  181.1 47.7 all-gather.4
where the time goes:
time: 253 us
  waiting for transfers between devices  209 us (83%)
  matrix products  14.7 us (6%)
  between operations  13.8 us (5%)
  local copies, waits for them, and re-layouts  12.5 us (5%)
    reduce_scatter x1, waiting for transfers between devices, local(): low_rank = lax.psum_scatter(whole, 'fsdp', scatter_dimension=0, tiled=True)  90.7 us
    all_gather x1, waiting for transfers between devices, local(): lax.all_gather(normalized, 'fsdp', axis=0, tiled=True)  46.4 us
    all_gather x1, waiting for transfers between devices, local(): lax.all_gather(projection, 'fsdp', axis=0, tiled=True)  42.8 us
    psum x1, waiting for transfers between devices, local(): whole = lax.psum(whole, 'dp')  28.8 us
    unnamed x13, local copies, waits for them, and re-layouts  12.5 us
    dot_general x1, matrix products, local(): lax.dot_general(grad_out, projected, contract, preferred_element_type=jnp...  7.64 us
    dot_general x1, matrix products, local(): lax.dot_general(projection, lax.all_gather(normalized, 'fsdp', axis=0, ti...  7.09 us
  transfers between devices with their start and end apart: 4, of which 4 were waited for; matrix products, arithmetic and copies ran while one was open for 1% of the time, Pallas kernels for 0%

commit v1 on v0

--- a/solution.py
+++ b/solution.py
@@ -4,6 +4,19 @@
 from jax.sharding import PartitionSpec as P
 
 STEP = 10
+
+
+def gather_around(x, axis, dim):
+    ways = lax.axis_size(axis)
+    up = [(d, (d + 1) % ways) for d in range(ways)]
+    down = [(d, (d - 1) % ways) for d in range(ways)]
+    earlier, later = ([x], [x])
+    for _ in range(ways // 2):
+        earlier.append(lax.ppermute(earlier[-1], axis, up))
+    for _ in range((ways - 1) // 2):
+        later.append(lax.ppermute(later[-1], axis, down))
+    line = jnp.concatenate([*earlier[::-1], *later[1:]], axis=dim)
+    return jnp.roll(line, (lax.axis_index(axis) - ways // 2) * x.shape[dim], axis=dim)
 
 
 def adam_step(low_rank, moment, second):
@@ -19,9 +32,7 @@
 
 def local(inputs, grad_out, projection, moment, second):
     projected = jnp.dot(
-        inputs,
-        lax.all_gather(projection, "fsdp", axis=0, tiled=True),
-        preferred_element_type=jnp.float32,
+        inputs, gather_around(projection, "fsdp", 0), preferred_element_type=jnp.float32
     ).astype(jnp.bfloat16)
     contract = (((0,), (0,)), ((), ()))
     whole = lax.dot_general(grad_out, projected, contract, preferred_element_type=jnp.float32)

time: 253 us -> 283 us (1.12)
  starting transfers between devices: 0.16 us -> 31.9 us
  waiting for transfers between devices: 209 us -> 186 us
  local copies, waits for them, and re-layouts: 12.5 us -> 33.2 us
    all_gather x1 -> x0, waiting for transfers between devices: 42.8 us -> none  [local(): lax.all_gather(projection, 'fsdp', axis=0, tiled=True)]
    ppermute x0 -> x15, starting transfers between devices: none -> 31.8 us  [the longest x7 31.2 us: gather_around(): later.append(lax.ppermute(later[-1], axis, down))]
    ppermute x0 -> x15, waiting for transfers between devices: none -> 20.6 us  [the longest x8 19.5 us: gather_around(): earlier.append(lax.ppermute(earlier[-1], axis, up))]
    unnamed x13 -> x44, local copies, waits for them, and re-layouts: 12.5 us -> 32.6 us
  transfers between devices with their start and end apart: 4 -> 18, of which waited for: 4 -> 17; matrix products, arithmetic and copies ran while one was open for 1% -> 4% of each run, Pallas kernels for 0% -> 0%
where the time goes in v1:
time: 283 us; the launch traced here: 282 us
  waiting for transfers between devices  186 us (66%)
  local copies, waits for them, and re-layouts  33.2 us (12%)
  starting transfers between devices  31.9 us (11%)
  matrix products  15.5 us (5%)
  between operations  13.8 us (5%)
    reduce_scatter x1, waiting for transfers between devices, local(): low_rank = lax.psum_scatter(whole, 'fsdp', scatter_dimension=0, tiled=True)  89.6 us
    all_gather x1, waiting for transfers between devices, local(): lax.all_gather(normalized, 'fsdp', axis=0, tiled=True)  46.6 us
    unnamed x44, local copies, waits for them, and re-layouts  32.6 us
    ppermute x7, starting transfers between devices, gather_around(): later.append(lax.ppermute(later[-1], axis, down))  31.2 us
    psum x1, waiting for transfers between devices, local(): whole = lax.psum(whole, 'dp')  28.8 us
    ppermute x8, waiting for transfers between devices, gather_around(): earlier.append(lax.ppermute(earlier[-1], axis, up))  19.5 us
    dot_general x1, matrix products, local(): lax.dot_general(grad_out, projected, contract, preferred_element_type=jnp...  8.41 us
    dot_general x1, matrix products, local(): lax.dot_general(projection, lax.all_gather(normalized, 'fsdp', axis=0, ti...  7.08 us
  transfers between devices with their start and end apart: 18, of which 17 were waited for; matrix products, arithmetic and copies ran while one was open for 4% of the time, Pallas kernels for 0%

profile of v1, /device:TPU:0, one launch (start us, length us, event | category | flops | bytes accessed | tf_op | source)
XLA Modules:
  0.0 282.0 jit_solution(16146803880195846584)
XLA Ops:
  7.2 0.5 collective-permute-start
  7.8 7.1 %collective-permute-done = bf16[256,128]{1,0:T(8,128)(2,1)S(1)} collective-permute-done((bf16[256,128]{1,0:T(8,128)(2,1)}, bf16[256,128]{1,0:T(8,128)(2,1)S(1)}, u32[]{:S(2)}, u32[]{:S(2)}) %collective-permute-start) | collective-permute-done | bytes 65568 | tf_op jit(solution)/shard_map/ppermute | solution.py:15
  14.9 4.4 %collective-permute-start.8 = (bf16[256,128]{1,0:T(8,128)(2,1)}, bf16[256,128]{1,0:T(8,128)(2,1)S(1)}, u32[]{:S(2)}, u32[]{:S(2)}) collective-permute-start(bf16[256,128]{1,0:T(8,128)(2,1)} %param.7), channel_id=1, source_target_pairs={{0,30},{2,0},{4,2},{6,4},{8,6},{10,8},{12,10},{14,12},{16,14},{18,... | collective-permute-start | bytes 196616 | tf_op jit(solution)/shard_map/ppermute | solution.py:17
  19.3 1.9 collective-permute-done.1
  21.3 0.3 collective-permute-done.8
  21.6 4.4 %collective-permute-start.9 = (bf16[256,128]{1,0:T(8,128)(2,1)S(1)}, bf16[256,128]{1,0:T(8,128)(2,1)S(1)}, u32[]{:S(2)}, u32[]{:S(2)}) collective-permute-start(bf16[256,128]{1,0:T(8,128)(2,1)S(1)} %collective-permute-done.8), channel_id=1, source_target_pairs={{0,30},{2,0},{4,2},{6,4},{8,6},{10,8},{12,10},{14,12},{16,14},{18,... | collective-permute-start | bytes 196616 | tf_op jit(solution)/shard_map/ppermute | solution.py:17
  25.9 1.7 collective-permute-done.2
  27.7 0.2 collective-permute-done.9
  27.8 4.5 %collective-permute-start.10 = (bf16[256,128]{1,0:T(8,128)(2,1)S(1)}, bf16[256,128]{1,0:T(8,128)(2,1)S(1)}, u32[]{:S(2)}, u32[]{:S(2)}) collective-permute-start(bf16[256,128]{1,0:T(8,128)(2,1)S(1)} %collective-permute-done.9), channel_id=1, source_target_pairs={{0,30},{2,0},{4,2},{6,4},{8,6},{10,8},{12,10},{14,12},{16,14},{18,... | collective-permute-start | bytes 196616 | tf_op jit(solution)/shard_map/ppermute | solution.py:17
  32.3 1.7 collective-permute-done.3
  34.1 0.2 collective-permute-done.10
  34.2 4.5 %collective-permute-start.11 = (bf16[256,128]{1,0:T(8,128)(2,1)S(1)}, bf16[256,128]{1,0:T(8,128)(2,1)S(1)}, u32[]{:S(2)}, u32[]{:S(2)}) collective-permute-start(bf16[256,128]{1,0:T(8,128)(2,1)S(1)} %collective-permute-done.10), channel_id=1, source_target_pairs={{0,30},{2,0},{4,2},{6,4},{8,6},{10,8},{12,10},{14,12},{16,14},{18,... | collective-permute-start | bytes 196616 | tf_op jit(solution)/shard_map/ppermute | solution.py:17
  38.7 1.7 collective-permute-done.4
  40.5 0.2 collective-permute-done.11
  40.6 4.5 %collective-permute-start.12 = (bf16[256,128]{1,0:T(8,128)(2,1)S(1)}, bf16[256,128]{1,0:T(8,128)(2,1)S(1)}, u32[]{:S(2)}, u32[]{:S(2)}) collective-permute-start(bf16[256,128]{1,0:T(8,128)(2,1)S(1)} %collective-permute-done.11), channel_id=1, source_target_pairs={{0,30},{2,0},{4,2},{6,4},{8,6},{10,8},{12,10},{14,12},{16,14},{18,... | collective-permute-start | bytes 196616 | tf_op jit(solution)/shard_map/ppermute | solution.py:17
  45.1 1.7 collective-permute-done.5
  47.0 4.5 %collective-permute-start.13 = (bf16[256,128]{1,0:T(8,128)(2,1)S(1)}, bf16[256,128]{1,0:T(8,128)(2,1)S(1)}, u32[]{:S(2)}, u32[]{:S(2)}) collective-permute-start(bf16[256,128]{1,0:T(8,128)(2,1)S(1)} %collective-permute-done.12), channel_id=1, source_target_pairs={{0,30},{2,0},{4,2},{6,4},{8,6},{10,8},{12,10},{14,12},{16,14},{18,... | collective-permute-start | bytes 196616 | tf_op jit(solution)/shard_map/ppermute | solution.py:17
  51.5 1.7 collective-permute-done.6
  53.2 0.2 collective-permute-done.13
  53.4 4.5 %collective-permute-start.14 = (bf16[256,128]{1,0:T(8,128)(2,1)S(1)}, bf16[256,128]{1,0:T(8,128)(2,1)S(1)}, u32[]{:S(2)}, u32[]{:S(2)}) collective-permute-start(bf16[256,128]{1,0:T(8,128)(2,1)S(1)} %collective-permute-done.13), channel_id=1, source_target_pairs={{0,30},{2,0},{4,2},{6,4},{8,6},{10,8},{12,10},{14,12},{16,14},{18,... | collective-permute-start | bytes 196616 | tf_op jit(solution)/shard_map/ppermute | solution.py:17
  57.9 1.7 collective-permute-done.7
  59.6 0.6 constant_dynamic-update-slice_fusion.31
  60.2 0.6 constant_dynamic-update-slice_fusion.30
  60.9 0.6 constant_dynamic-update-slice_fusion.29
  61.5 0.6 constant_dynamic-update-slice_fusion.28
  62.1 0.6 constant_dynamic-update-slice_fusion.27
  62.7 0.6 constant_dynamic-update-slice_fusion.26
  63.4 0.6 constant_dynamic-update-slice_fusion.25
  64.0 0.6 constant_dynamic-update-slice_fusion.24
  64.6 1.5 constant_dynamic-update-slice_fusion.23
  66.1 0.6 constant_dynamic-update-slice_fusion.22
  66.7 0.6 constant_dynamic-update-slice_fusion.21
  67.3 0.6 constant_dynamic-update-slice_fusion.20
  67.9 0.6 constant_dynamic-update-slice_fusion.19
  68.6 0.6 constant_dynamic-update-slice_fusion.18
  69.2 0.6 constant_dynamic-update-slice_fusion.17
  69.8 0.6 constant_dynamic-update-slice_fusion.16
  70.4 0.6 constant_dynamic-update-slice_fusion.15
  71.1 0.6 constant_dynamic-update-slice_fusion.14
  71.7 0.6 constant_dynamic-update-slice_fusion.13
  72.3 0.6 constant_dynamic-update-slice_fusion.12
  72.9 0.6 constant_dynamic-update-slice_fusion.11
  73.5 0.6 constant_dynamic-update-slice_fusion.10
  74.2 0.6 constant_dynamic-update-slice_fusion.9
  74.8 0.6 constant_dynamic-update-slice_fusion.8
  75.4 0.6 constant_dynamic-update-slice_fusion.7
  76.0 0.6 constant_dynamic-update-slice_fusion.6
  76.7 0.6 constant_dynamic-update-slice_fusion.5
  77.3 0.6 constant_dynamic-update-slice_fusion.4
  77.9 0.6 constant_dynamic-update-slice_fusion.3
  78.5 0.6 constant_dynamic-update-slice_fusion.2
  79.1 0.6 constant_dynamic-update-slice_fusion.1
  79.8 0.6 constant_dynamic-update-slice_fusion
  80.4 8.4 %convolution_bitcast_fusion = f32[14336,128]{0,1:T(8,128)} fusion(bf16[192,14336]{1,0:T(8,128)(2,1)} %param.6, bf16[192,4096]{1,0:T(8,128)(2,1)S(1)} %copy-done, bf16[8192,128]{1,0:T(8,128)(2,1)} %constant_dynamic-update-slice_fusion, s32[]{:T(128)S(6)} %select_n.14), kind=kOutput, calls=%fused_computation.2 | convolution fusion | flops 905994240 | bytes 15466500 | tf_op jit(solution)/shard_map/dot_general | solution.py:38
  88.9 89.6 %reduce-scatter.2.cloned.1.call-done = f32[896,128]{0,1:T(8,128)} async-done(((f32[14336,128]{0,1:T(8,128)}), f32[896,128]{0,1:T(8,128)}) %reduce-scatter.2.cloned.1.call-update) | async-done | bytes 458768 | tf_op jit(solution)/shard_map/reduce_scatter | solution.py:40
  178.5 0.2 copy.8
  178.7 0.2 copy.9
  178.9 28.8 %all-reduce.2.cloned.1.call-done = f32[896,128]{0,1:T(8,128)} async-done(((f32[896,128]{0,1:T(8,128)}), f32[896,128]{0,1:T(8,128)}) %all-reduce.2.cloned.1.call-update) | async-done | bytes 458768 | tf_op jit(solution)/shard_map/psum | solution.py:39
  207.8 2.0 divide_convert_fusion
  209.8 1.0 copy.11
  210.8 1.0 copy.12
  211.7 46.6 %all-gather.2.cloned.1.call-done = bf16[14336,128]{0,1:T(8,128)(2,1)} async-done(((bf16[896,128]{0,1:T(8,128)(2,1)}), bf16[14336,128]{0,1:T(8,128)(2,1)}) %all-gather.2.cloned.1.call-update) | async-done | bytes 3670032 | tf_op jit(solution)/shard_map/all_gather | solution.py:45
  258.3 7.1 %fusion = bf16[256,14336]{0,1:T(8,128)(2,1)} fusion(bf16[14336,128]{0,1:T(8,128)(2,1)} %all-gather.2.cloned.1.call-done, bf16[256,128]{1,0:T(8,128)(2,1)S(1)} %copy-done.1), kind=kOutput, calls=%fused_computation.1 | convolution fusion | flops 943194112 | bytes 11075584 | tf_op jit(solution)/shard_map/dot_general | solution.py:43
  265.4 10.1 %copy.10 = bf16[256,14336]{1,0:T(8,128)(2,1)} copy(bf16[256,14336]{0,1:T(8,128)(2,1)} %fusion) | data formatting | bytes 14680064
  (23 shorter events, 0.4 us)
Async XLA Ops:
  7.2 73.2 %copy-start = (bf16[192,4096]{1,0:T(8,128)(2,1)S(1)}, bf16[192,4096]{1,0:T(8,128)(2,1)}, u32[]{:S(2)}) copy-start(bf16[192,4096]{1,0:T(8,128)(2,1)} %param.5) | copy-start | bytes 4718596
  7.2 68.2 %copy-start.1 = (bf16[256,128]{1,0:T(8,128)(2,1)S(1)}, bf16[256,128]{1,0:T(8,128)(2,1)}, u32[]{:S(2)}) copy-start(bf16[256,128]{1,0:T(8,128)(2,1)} %param.7) | copy-start | bytes 196612
  7.2 171.3 %reduce-scatter.2.cloned.1.call-start = ((), (), s32[]{:S(2)}) async-start(), calls=%async_computation.2 | async-start | bytes 7798784 | tf_op jit(solution)/shard_map/reduce_scatter | solution.py:40
  7.2 7.7 %collective-permute-start = (bf16[256,128]{1,0:T(8,128)(2,1)}, bf16[256,128]{1,0:T(8,128)(2,1)S(1)}, u32[]{:S(2)}, u32[]{:S(2)}) collective-permute-start(bf16[256,128]{1,0:T(8,128)(2,1)} %param.7), channel_id=1, source_target_pairs={{0,2},{2,4},{4,6},{6,8},{8,10},{10,12},{12,14},{14,16},{16,18},{18... | collective-permute-start | bytes 196616 | tf_op jit(solution)/shard_map/ppermute | solution.py:15
  14.9 6.4 %collective-permute-start.1 = (bf16[256,128]{1,0:T(8,128)(2,1)S(1)}, bf16[256,128]{1,0:T(8,128)(2,1)S(1)}, u32[]{:S(2)}, u32[]{:S(2)}) collective-permute-start(bf16[256,128]{1,0:T(8,128)(2,1)S(1)} %collective-permute-done), channel_id=1, source_target_pairs={{0,2},{2,4},{4,6},{6,8},{8,10},{10,12},{12,14},{14,16},{16,18},{18... | collective-permute-start | bytes 196616 | tf_op jit(solution)/shard_map/ppermute | solution.py:15
  14.9 6.7 %collective-permute-start.8 = (bf16[256,128]{1,0:T(8,128)(2,1)}, bf16[256,128]{1,0:T(8,128)(2,1)S(1)}, u32[]{:S(2)}, u32[]{:S(2)}) collective-permute-start(bf16[256,128]{1,0:T(8,128)(2,1)} %param.7), channel_id=1, source_target_pairs={{0,30},{2,0},{4,2},{6,4},{8,6},{10,8},{12,10},{14,12},{16,14},{18,... | collective-permute-start | bytes 196616 | tf_op jit(solution)/shard_map/ppermute | solution.py:17
  21.3 6.4 %collective-permute-start.2 = (bf16[256,128]{1,0:T(8,128)(2,1)S(1)}, bf16[256,128]{1,0:T(8,128)(2,1)S(1)}, u32[]{:S(2)}, u32[]{:S(2)}) collective-permute-start(bf16[256,128]{1,0:T(8,128)(2,1)S(1)} %collective-permute-done.1), channel_id=1, source_target_pairs={{0,2},{2,4},{4,6},{6,8},{8,10},{10,12},{12,14},{14,16},{16,18},{18... | collective-permute-start | bytes 196616 | tf_op jit(solution)/shard_map/ppermute | solution.py:15
  21.6 6.3 %collective-permute-start.9 = (bf16[256,128]{1,0:T(8,128)(2,1)S(1)}, bf16[256,128]{1,0:T(8,128)(2,1)S(1)}, u32[]{:S(2)}, u32[]{:S(2)}) collective-permute-start(bf16[256,128]{1,0:T(8,128)(2,1)S(1)} %collective-permute-done.8), channel_id=1, source_target_pairs={{0,30},{2,0},{4,2},{6,4},{8,6},{10,8},{12,10},{14,12},{16,14},{18,... | collective-permute-start | bytes 196616 | tf_op jit(solution)/shard_map/ppermute | solution.py:17
  27.7 6.4 %collective-permute-start.3 = (bf16[256,128]{1,0:T(8,128)(2,1)S(1)}, bf16[256,128]{1,0:T(8,128)(2,1)S(1)}, u32[]{:S(2)}, u32[]{:S(2)}) collective-permute-start(bf16[256,128]{1,0:T(8,128)(2,1)S(1)} %collective-permute-done.2), channel_id=1, source_target_pairs={{0,2},{2,4},{4,6},{6,8},{8,10},{10,12},{12,14},{14,16},{16,18},{18... | collective-permute-start | bytes 196616 | tf_op jit(solution)/shard_map/ppermute | solution.py:15
  27.8 6.4 %collective-permute-start.10 = (bf16[256,128]{1,0:T(8,128)(2,1)S(1)}, bf16[256,128]{1,0:T(8,128)(2,1)S(1)}, u32[]{:S(2)}, u32[]{:S(2)}) collective-permute-start(bf16[256,128]{1,0:T(8,128)(2,1)S(1)} %collective-permute-done.9), channel_id=1, source_target_pairs={{0,30},{2,0},{4,2},{6,4},{8,6},{10,8},{12,10},{14,12},{16,14},{18,... | collective-permute-start | bytes 196616 | tf_op jit(solution)/shard_map/ppermute | solution.py:17
  34.1 6.4 %collective-permute-start.4 = (bf16[256,128]{1,0:T(8,128)(2,1)S(1)}, bf16[256,128]{1,0:T(8,128)(2,1)S(1)}, u32[]{:S(2)}, u32[]{:S(2)}) collective-permute-start(bf16[256,128]{1,0:T(8,128)(2,1)S(1)} %collective-permute-done.3), channel_id=1, source_target_pairs={{0,2},{2,4},{4,6},{6,8},{8,10},{10,12},{12,14},{14,16},{16,18},{18... | collective-permute-start | bytes 196616 | tf_op jit(solution)/shard_map/ppermute | solution.py:15
  34.2 6.4 %collective-permute-start.11 = (bf16[256,128]{1,0:T(8,128)(2,1)S(1)}, bf16[256,128]{1,0:T(8,128)(2,1)S(1)}, u32[]{:S(2)}, u32[]{:S(2)}) collective-permute-start(bf16[256,128]{1,0:T(8,128)(2,1)S(1)} %collective-permute-done.10), channel_id=1, source_target_pairs={{0,30},{2,0},{4,2},{6,4},{8,6},{10,8},{12,10},{14,12},{16,14},{18,... | collective-permute-start | bytes 196616 | tf_op jit(solution)/shard_map/ppermute | solution.py:17
  40.5 6.4 %collective-permute-start.5 = (bf16[256,128]{1,0:T(8,128)(2,1)S(1)}, bf16[256,128]{1,0:T(8,128)(2,1)S(1)}, u32[]{:S(2)}, u32[]{:S(2)}) collective-permute-start(bf16[256,128]{1,0:T(8,128)(2,1)S(1)} %collective-permute-done.4), channel_id=1, source_target_pairs={{0,2},{2,4},{4,6},{6,8},{8,10},{10,12},{12,14},{14,16},{16,18},{18... | collective-permute-start | bytes 196616 | tf_op jit(solution)/shard_map/ppermute | solution.py:15
  40.6 6.4 %collective-permute-start.12 = (bf16[256,128]{1,0:T(8,128)(2,1)S(1)}, bf16[256,128]{1,0:T(8,128)(2,1)S(1)}, u32[]{:S(2)}, u32[]{:S(2)}) collective-permute-start(bf16[256,128]{1,0:T(8,128)(2,1)S(1)} %collective-permute-done.11), channel_id=1, source_target_pairs={{0,30},{2,0},{4,2},{6,4},{8,6},{10,8},{12,10},{14,12},{16,14},{18,... | collective-permute-start | bytes 196616 | tf_op jit(solution)/shard_map/ppermute | solution.py:17
  46.8 6.4 %collective-permute-start.6 = (bf16[256,128]{1,0:T(8,128)(2,1)S(1)}, bf16[256,128]{1,0:T(8,128)(2,1)S(1)}, u32[]{:S(2)}, u32[]{:S(2)}) collective-permute-start(bf16[256,128]{1,0:T(8,128)(2,1)S(1)} %collective-permute-done.5), channel_id=1, source_target_pairs={{0,2},{2,4},{4,6},{6,8},{8,10},{10,12},{12,14},{14,16},{16,18},{18... | collective-permute-start | bytes 196616 | tf_op jit(solution)/shard_map/ppermute | solution.py:15
  47.0 6.4 %collective-permute-start.13 = (bf16[256,128]{1,0:T(8,128)(2,1)S(1)}, bf16[256,128]{1,0:T(8,128)(2,1)S(1)}, u32[]{:S(2)}, u32[]{:S(2)}) collective-permute-start(bf16[256,128]{1,0:T(8,128)(2,1)S(1)} %collective-permute-done.12), channel_id=1, source_target_pairs={{0,30},{2,0},{4,2},{6,4},{8,6},{10,8},{12,10},{14,12},{16,14},{18,... | collective-permute-start | bytes 196616 | tf_op jit(solution)/shard_map/ppermute | solution.py:17
  53.2 6.4 %collective-permute-start.7 = (bf16[256,128]{1,0:T(8,128)(2,1)S(1)}, bf16[256,128]{1,0:T(8,128)(2,1)S(1)}, u32[]{:S(2)}, u32[]{:S(2)}) collective-permute-start(bf16[256,128]{1,0:T(8,128)(2,1)S(1)} %collective-permute-done.6), channel_id=1, source_target_pairs={{0,2},{2,4},{4,6},{6,8},{8,10},{10,12},{12,14},{14,16},{16,18},{18... | collective-permute-start | bytes 196616 | tf_op jit(solution)/shard_map/ppermute | solution.py:15
  53.4 16.4 %collective-permute-start.14 = (bf16[256,128]{1,0:T(8,128)(2,1)S(1)}, bf16[256,128]{1,0:T(8,128)(2,1)S(1)}, u32[]{:S(2)}, u32[]{:S(2)}) collective-permute-start(bf16[256,128]{1,0:T(8,128)(2,1)S(1)} %collective-permute-done.13), channel_id=1, source_target_pairs={{0,30},{2,0},{4,2},{6,4},{8,6},{10,8},{12,10},{14,12},{16,14},{18,... | collective-permute-start | bytes 196616 | tf_op jit(solution)/shard_map/ppermute | solution.py:17
  88.8 89.7 %copy-start.2 = (f32[896,128]{1,0:T(8,128)S(1)}, f32[896,128]{1,0:T(8,128)}, u32[]{:S(2)}) copy-start(f32[896,128]{1,0:T(8,128)} %param.8) | copy-start | bytes 1376260
  88.8 89.9 %copy-start.3 = (f32[896,128]{1,0:T(8,128)S(1)}, f32[896,128]{1,0:T(8,128)}, u32[]{:S(2)}) copy-start(f32[896,128]{1,0:T(8,128)} %param.9) | copy-start | bytes 1376260
  88.8 118.9 %all-reduce.2.cloned.1.call-start = ((), (), s32[]{:S(2)}) async-start(), calls=%async_computation.3 | async-start | bytes 917504 | tf_op jit(solution)/shard_map/psum | solution.py:39
  178.5 79.8 %all-gather.2.cloned.1.call-start = ((), (), s32[]{:S(2)}) async-start(), calls=%async_computation.1 | async-start | bytes 3899392 | tf_op jit(solution)/shard_map/all_gather | solution.py:45
Sparse Core Ops, SparseCore 0:
  89.0 89.4 reduce-scatter.1
  180.7 26.9 all-reduce.1
  210.5 47.7 all-gather.1
